TPU v7x, 32 devices: a whole 2x2x4 slice. The times are simulated.
32 devices in a mesh: seq: 8 (over z, core), head: 4 (over y, x).
Axes of the slice: x: 2, y: 2, z: 4, core: 2. Of those that a mesh axis runs over, the one named last changes fastest.
Arguments:
- grad_output: bfloat16 [8192, 4096], P('seq', 'head'), may hold values from -6 to 6
- out_weight: bfloat16 [4096, 8192], P('seq', 'head'), may hold values from -0.0625 to 0.0625
- ssd_out: bfloat16 [8192, 8192], P('seq', 'head'), may hold values from -520 to 520
- gate: bfloat16 [8192, 8192], P('seq', 'head'), may hold values from -5 to 5
- norm_weight: float32 [8192], P('head'), may hold values from 0.5 to 1.5
- time_step: float32 [128, 8192], P('head', 'seq'), may hold values from 0.01 to 0.1
- log_decay: float32 [128, 8192], P('head', 'seq'), may hold values from -0.7 to 0
- state_in: bfloat16 [8192, 8, 128], P('seq'), may hold values from -1.796875 to 1.796875
- state_out: bfloat16 [8192, 8, 128], P('seq'), may hold values from -1.796875 to 1.796875
- skip: float32 [128], P('head'), may hold values from 0.5 to 1.5
Outputs:
- grad_x: bfloat16 [8192, 8192], P('seq', 'head')
- grad_gate: bfloat16 [8192, 8192], P('seq', 'head')
- grad_out_weight: float32 [4096, 8192], P('seq', 'head')
All inputs are finite; a program needn't handle non-finite values.
Results may differ from a plain program's by a relative error of at most 0.014.
Values may be sent and summed in bfloat16 or wider, within the bound.
A program may use at most 192 MiB of HBM per device.

v0:
```python
import math
import jax
import jax.numpy as jnp
from jax import lax
from jax.sharding import PartitionSpec as P

HEADS = 128
GROUPS = 8
BLOCK_LEN = 256
epsilon = 1e-05


def shifted(x, axis, by):
    size = lax.axis_size(axis)
    pairs = [(i, i + by) for i in range(size) if 0 <= i + by < size]
    return lax.ppermute(x, axis, pairs)


def on_device(
    grad_output,
    out_weight,
    ssd_out,
    gate,
    norm_weight,
    time_step,
    log_decay,
    state_in,
    state_out,
    skip,
):
    tok_rows = ssd_out.shape[0]
    local_width = ssd_out.shape[1]
    total_width = local_width * lax.axis_size("head")
    full_grad = lax.all_gather(grad_output, "head", axis=1, tiled=True)
    values = ssd_out.astype(jnp.float32)
    gate_values = gate.astype(jnp.float32)
    sigmoid_gate = jax.nn.sigmoid(gate_values)
    silu_gate = gate_values * sigmoid_gate
    gated_values = values * silu_gate
    local_squares = jnp.sum(gated_values * gated_values, axis=1)
    squares = lax.psum(local_squares, "head")
    columns = full_grad
    normed_grad = jnp.dot(
        columns,
        lax.all_gather(out_weight, "seq", axis=0, tiled=True),
        preferred_element_type=jnp.float32,
    )
    weighted = lax.psum(jnp.sum(norm_weight * normed_grad * gated_values, axis=1), "head")
    inverse_rms = lax.rsqrt(squares[:, None] / total_width + epsilon)
    normed = (gated_values * inverse_rms * norm_weight).astype(jnp.bfloat16)
    gated_grad = (
        inverse_rms * norm_weight * normed_grad
        - gated_values * inverse_rms**3 * weighted[:, None] / total_width
    )
    grad_gate = (
        gated_grad * values * sigmoid_gate * (1.0 + gate_values * (1.0 - sigmoid_gate))
    ).astype(jnp.bfloat16)
    grad_ssd = (gated_grad * silu_gate).astype(jnp.bfloat16)
    columns = full_grad
    weight_sum = lax.psum_scatter(
        lax.dot_general(
            columns, normed, (((0,), (0,)), ((), ())), preferred_element_type=jnp.float32
        ),
        "seq",
        scatter_dimension=0,
        tiled=True,
    )
    grad_out_weight = weight_sum * (1.0 / math.sqrt(tok_rows * lax.axis_size("seq")))
    heads_here = time_step.shape[0]
    head_width = local_width // heads_here
    blocks = tok_rows // BLOCK_LEN
    state_width = state_in.shape[2]
    group_count = state_in.shape[1]
    first_head = lax.axis_index("head") * heads_here
    head_ids = first_head + jnp.arange(heads_here, dtype=jnp.int32)
    group_ids = head_ids // (HEADS // GROUPS)
    group_pick = (group_ids[:, None] == jnp.arange(group_count, dtype=jnp.int32)[None, :]).astype(
        jnp.bfloat16
    )
    b_heads = jnp.einsum(
        "tgn,hg->htn", state_in, group_pick, preferred_element_type=jnp.float32
    ).astype(jnp.bfloat16)
    b_heads = b_heads.reshape(heads_here, blocks, BLOCK_LEN, state_width)
    c_heads = jnp.einsum(
        "tgn,hg->htn", state_out, group_pick, preferred_element_type=jnp.float32
    ).astype(jnp.bfloat16)
    c_heads = c_heads.reshape(heads_here, blocks, BLOCK_LEN, state_width)
    grad_heads = grad_ssd.reshape(tok_rows, heads_here, head_width).transpose(1, 0, 2)
    grad_heads = grad_heads.reshape(heads_here, blocks, BLOCK_LEN, head_width)
    cumulative = jnp.cumsum(log_decay.reshape(heads_here, blocks, BLOCK_LEN), axis=2)
    block_total = cumulative[..., -1]
    sequence_indices = jnp.arange(BLOCK_LEN)
    upper_mask = sequence_indices[None, :] >= sequence_indices[:, None]
    scores = jnp.einsum("hktn,hksn->hkts", b_heads, c_heads, preferred_element_type=jnp.float32)
    log_gap = cumulative[..., None, :] - cumulative[..., :, None]
    block_weights = jnp.where(upper_mask, scores * jnp.exp(jnp.minimum(log_gap, 0.0)), 0.0).astype(
        jnp.bfloat16
    )
    within = jnp.einsum(
        "hkts,hksp->hktp", block_weights, grad_heads, preferred_element_type=jnp.float32
    )
    grad_float = grad_heads.astype(jnp.float32)
    scaled = (jnp.exp(cumulative)[..., None] * grad_float).astype(jnp.bfloat16)
    block_state = jnp.einsum("hksp,hksn->hkpn", scaled, c_heads, preferred_element_type=jnp.float32)

    def fold_block(carried, inputs):
        state_now, total_now = inputs
        return (state_now + jnp.exp(total_now)[:, None, None] * carried, carried)

    zero_state = jnp.zeros((heads_here, head_width, state_width), jnp.float32)
    summary, inside = lax.scan(
        fold_block, zero_state, (block_state.transpose(1, 0, 2, 3), block_total.T), reverse=True
    )
    decay_total = jnp.exp(jnp.sum(block_total, axis=1))
    tail_decay = jnp.exp(
        jnp.sum(block_total, axis=1, keepdims=True) - jnp.cumsum(block_total, axis=1)
    )

    def pass_back(relay_turn, carried_state):
        return shifted(
            (summary + decay_total[:, None, None] * carried_state).astype(jnp.bfloat16), "seq", -1
        ).astype(jnp.float32)

    remote = lax.fori_loop(0, lax.axis_size("seq") - 1, pass_back, zero_state)
    full_states = inside.transpose(1, 0, 2, 3) + tail_decay[..., None, None] * remote[:, None]
    carry_low = full_states.astype(jnp.bfloat16)
    across = jnp.einsum("hkpn,hktn->hktp", carry_low, b_heads, preferred_element_type=jnp.float32)
    across = across * jnp.exp(block_total[..., None] - cumulative)[..., None]
    step_sizes = time_step.reshape(heads_here, blocks, BLOCK_LEN)
    grad_head = step_sizes[..., None] * (within + across) + skip[:, None, None, None] * grad_float
    grad_x = (
        grad_head.reshape(heads_here, tok_rows, head_width)
        .transpose(1, 0, 2)
        .reshape(tok_rows, local_width)
    )
    return (grad_x.astype(jnp.bfloat16), grad_gate, grad_out_weight)


def solution(mesh):
    return jax.shard_map(
        on_device,
        mesh=mesh,
        in_specs=(
            P("seq", "head"),
            P("seq", "head"),
            P("seq", "head"),
            P("seq", "head"),
            P("head"),
            P("head", "seq"),
            P("head", "seq"),
            P("seq", None, None),
            P("seq", None, None),
            P("head"),
        ),
        out_specs=(P("seq", "head"), P("seq", "head"), P("seq", "head")),
        check_vma=False,
    )
```

profile of v0, /device:TPU:0, one launch (start us, length us, event | category | flops | bytes accessed | tf_op | source)
XLA Modules:
  0.0 695.3 jit_solution(3840516232914218780)
XLA Ops:
  8.7 91.3 %all-gather.3.cloned.1.call-done = bf16[1024,4096]{1,0:T(8,128)(2,1)} async-done(((bf16[1024,1024]{1,0:T(8,128)(2,1)}), bf16[1024,4096]{1,0:T(8,128)(2,1)}) %all-gather.3.cloned.1.call-update) | async-done | bytes 8388624 | tf_op jit(solution)/shard_map/all_gather | solution.py:34
  100.1 152.7 %all-gather.5.cloned.1.call-done = bf16[4096,2048]{1,0:T(8,128)(2,1)} async-done(((bf16[512,2048]{1,0:T(8,128)(2,1)}), bf16[4096,2048]{1,0:T(8,128)(2,1)}) %all-gather.5.cloned.1.call-update) | async-done | bytes 16777232 | tf_op jit(solution)/shard_map/all_gather | solution.py:45
  252.8 27.2 %multiply_reduce_fusion.1 = (f32[1024]{0:T(1024)S(1)}, f32[1024]{0:T(1024)S(1)}, f32[1024,2048]{1,0:T(8,128)}) fusion(bf16[1024,2048]{1,0:T(8,128)(2,1)} %param.16, bf16[1024,2048]{1,0:T(8,128)(2,1)} %param.17, f32[2048]{0:T(1024)} %param.18, bf16[1024,4096]{1,0:T(8,128)(2,1)} %all-gather.3.cloned.1.call-done, ...), kind=kOutput, calls=%fused_computation.34 | convolution fusion | flops 17205035008 | bytes 41959424 | tf_op jit(solution)/shard_map/dot_general | solution.py:43
  279.9 10.5 %all-reduce = (f32[1024]{0:T(1024)}, f32[1024]{0:T(1024)S(1)}) all-reduce(f32[1024]{0:T(1024)S(1)} %get-tuple-element.190, f32[1024]{0:T(1024)S(1)} %get-tuple-element.189), channel_id=1, replica_groups=mesh['seq'=8,'head'=4] {'head'}, use_global_device_ids=true, to_apply=%region_5.6 | all-reduce | flops 2048 | bytes 16384 | tf_op jit(solution)/shard_map/psum | solution.py:48
  290.5 26.7 %convolution_bitcast_fusion = f32[4096,2048]{0,1:T(8,128)} fusion(bf16[1024,4096]{1,0:T(8,128)(2,1)} %all-gather.3.cloned.1.call-done, bf16[1024,2048]{1,0:T(8,128)(2,1)} %param.16, f32[2048]{0:T(1024)S(1)} %copy-done.11, f32[1024]{0:T(1024)S(1)} %get-tuple-element.217, bf16[1024,2048]{1,0:T(8,128)(2,1)} %param.17), kind=kOutput, calls=%fused_computation.9 | convolution fusion | flops 17200840704 | bytes 50343936 | tf_op jit(solution)/shard_map/dot_general | solution.py:61
  325.9 5.5 convolution_convert_fusion.1
  331.4 5.3 convolution_convert_fusion
  337.7 9.0 %fusion.10 = (bf16[1024,2048]{1,0:T(8,128)(2,1)}, bf16[1024,2048]{1,0:T(8,128)(2,1)}) fusion(bf16[1024,2048]{1,0:T(8,128)(2,1)S(1)} %copy-done.3, bf16[1024,2048]{1,0:T(8,128)(2,1)S(1)} %copy-done.4, f32[1024]{0:T(1024)S(1)} %copy-done.14, f32[1024,2048]{1,0:T(8,128)S(1)} %bitcast.75, f32[1024]{0:T(1024)S(1)} %get-tuple-element.218, f32[2048]{0:T(1024)S(1)} %copy-done.12, ...), kind=kLoop, calls=%fused_computation.22 | loop fusion | flops 46137344 | bytes 25186304 | tf_op jit(solution)/shard_map/convert_element_type | solution.py:57
  346.7 7.0 %copy.45 = bf16[1024,2048]{0,1:T(8,128)(2,1)} copy(bf16[1024,2048]{1,0:T(8,128)(2,1)} %get-tuple-element.214) | data formatting | bytes 8388608 | tf_op jit(solution)/shard_map/convert_element_type | solution.py:58
  353.7 16.3 %fusion.39 = f32[4,32,64,128]{3,2,0,1:T(8,128)} fusion(bf16[32,4,256,128]{3,0,2,1:T(8,128)(2,1)} %bitcast.76, f32[32,4,256]{2,1,0:T(4,128)S(1)} %copy-done.8, bf16[32,8,4,8,256]{4,3,2,1,0:T(8,128)(2,1)} %bitcast.78), kind=kOutput, calls=%fused_computation.52 | convolution fusion | flops 543162368 | bytes 16908288 | tf_op jit(solution)/shard_map/hksp,hksn->hkpn/dot_general | solution.py:104
  372.5 10.1 %while.28 = (s32[]{:T(128)}, f32[32,64,128]{2,1,0:T(8,128)S(1)}, f32[4,32,64,128]{3,2,1,0:T(8,128)}, f32[4,32,64,128]{3,2,0,1:T(8,128)}, f32[4,32]{1,0:T(4,128)S(1)}, /*index=5*/s32[]{:T(128)}, s32[]{:T(128)}, s32[]{:T(128)}) while((s32[]{:T(128)}, f32[32,64,128]{2,1,0:T(8,128)S(1)}, f32[4,32,64,128]{3,2,1,0:T(8,128)}, ...), condition=%wide.region_7.8_spmd.clone, body=%wide.region_6.7_spmd.clone.sunk | while | flops 1048580 | bytes 5243392 | solution.py:111
  382.7 138.0 %while.29 = (s32[]{:T(128)}, f32[32,64,128]{2,1,0:T(8,128)S(1)}, f32[32]{0:T(128)S(1)}, f32[32,64,128]{2,1,0:T(8,128)S(1)}, s32[]{:T(128)}, /*index=5*/s32[]{:T(128)}) while((s32[]{:T(128)}, f32[32,64,128]{2,1,0:T(8,128)S(1)}, f32[32]{0:T(128)S(1)}, f32[32,64,128]{2,1,0:T(8,128)S(1)}, s32[]{:T(128)}, /*index=5*/s32[]{:T(128)}) %tuple.85), condition=%wide.region_11.12_spmd.clone, body=%wide.region_10.11_spmd.clone.sunk | while | flops 1310723 | bytes 6291703 | solution.py:124
  388.4 19.1 %collective-permute-done = bf16[32,64,128]{2,1,0:T(8,128)(2,1)S(1)} collective-permute-done((bf16[32,64,128]{2,1,0:T(8,128)(2,1)S(1)}, bf16[32,64,128]{2,1,0:T(8,128)(2,1)S(1)}, u32[]{:S(2)}, u32[]{:S(2)}) %collective-permute-start) | collective-permute-done | bytes 524320 | tf_op jit(solution)/shard_map/while/body/eval_jaxpr/ppermute | solution.py:16
  409.1 20.8 %collective-permute-done = bf16[32,64,128]{2,1,0:T(8,128)(2,1)S(1)} collective-permute-done((bf16[32,64,128]{2,1,0:T(8,128)(2,1)S(1)}, bf16[32,64,128]{2,1,0:T(8,128)(2,1)S(1)}, u32[]{:S(2)}, u32[]{:S(2)}) %collective-permute-start) | collective-permute-done | bytes 524320 | tf_op jit(solution)/shard_map/while/body/eval_jaxpr/ppermute | solution.py:16
  431.6 21.0 %collective-permute-done = bf16[32,64,128]{2,1,0:T(8,128)(2,1)S(1)} collective-permute-done((bf16[32,64,128]{2,1,0:T(8,128)(2,1)S(1)}, bf16[32,64,128]{2,1,0:T(8,128)(2,1)S(1)}, u32[]{:S(2)}, u32[]{:S(2)}) %collective-permute-start) | collective-permute-done | bytes 524320 | tf_op jit(solution)/shard_map/while/body/eval_jaxpr/ppermute | solution.py:16
  454.2 21.0 %collective-permute-done = bf16[32,64,128]{2,1,0:T(8,128)(2,1)S(1)} collective-permute-done((bf16[32,64,128]{2,1,0:T(8,128)(2,1)S(1)}, bf16[32,64,128]{2,1,0:T(8,128)(2,1)S(1)}, u32[]{:S(2)}, u32[]{:S(2)}) %collective-permute-start) | collective-permute-done | bytes 524320 | tf_op jit(solution)/shard_map/while/body/eval_jaxpr/ppermute | solution.py:16
  476.8 21.0 %collective-permute-done = bf16[32,64,128]{2,1,0:T(8,128)(2,1)S(1)} collective-permute-done((bf16[32,64,128]{2,1,0:T(8,128)(2,1)S(1)}, bf16[32,64,128]{2,1,0:T(8,128)(2,1)S(1)}, u32[]{:S(2)}, u32[]{:S(2)}) %collective-permute-start) | collective-permute-done | bytes 524320 | tf_op jit(solution)/shard_map/while/body/eval_jaxpr/ppermute | solution.py:16
  499.5 21.0 %collective-permute-done = bf16[32,64,128]{2,1,0:T(8,128)(2,1)S(1)} collective-permute-done((bf16[32,64,128]{2,1,0:T(8,128)(2,1)S(1)}, bf16[32,64,128]{2,1,0:T(8,128)(2,1)S(1)}, u32[]{:S(2)}, u32[]{:S(2)}) %collective-permute-start) | collective-permute-done | bytes 524320 | tf_op jit(solution)/shard_map/while/body/eval_jaxpr/ppermute | solution.py:16
  520.8 17.2 %fusion.22 = f32[32,4,256,64]{2,3,1,0:T(8,128)} fusion(bf16[32,4,256,128]{3,0,2,1:T(8,128)(2,1)} %bitcast.71, f32[4,32,64,128]{3,2,1,0:T(8,128)} %get-tuple-element.129, f32[32,64,128]{2,1,0:T(8,128)S(1)} %get-tuple-element.131, f32[32,4]{0,1:T(4,128)S(1)} %copy-done.13), kind=kOutput, calls=%fused_computation.38 | convolution fusion | flops 540016640 | bytes 22020608 | tf_op jit(solution)/shard_map/hkpn,hktn->hktp/dot_general | solution.py:127
  538.0 21.0 %fusion.44 = bf16[32,4,8,8,256]{4,3,2,1,0:T(8,128)(2,1)} fusion(bf16[32,8,4,8,256]{4,3,2,1,0:T(8,128)(2,1)} %bitcast.79, f32[32]{0:T(128)S(1)} %copy-done.16, f32[32,4,256,64]{2,3,1,0:T(8,128)} %fusion.22, f32[32,4,256]{2,1,0:T(4,128)S(1)} %copy.53, f32[32,4,256]{2,1,0:T(4,128)S(1)} %copy.43, pred[256,256]{1,0:T(8,128)(4,1)S(1)} %copy-done.9, ...), kind=kOutput, calls=%fused_computation.53 | convolution fusion | flops 3277848576 | bytes 34013312 | tf_op jit(solution)/shard_map/hkts,hksp->hktp/dot_general | solution.py:99
  558.9 4.8 copy.60
  563.8 6.6 copy.55
  570.4 108.2 %reduce-scatter.2.cloned.1.call-done = f32[512,2048]{0,1:T(8,128)} async-done(((f32[4096,2048]{0,1:T(8,128)}), f32[512,2048]{0,1:T(8,128)}) %reduce-scatter.2.cloned.1.call-update) | async-done | bytes 4194320 | tf_op jit(solution)/shard_map/reduce_scatter | solution.py:60
  683.2 5.3 copy.56
  (102 shorter events, 42.1 us)
Async XLA Ops:
  7.2 318.7 %copy-start = (bf16[1024,8,128]{2,1,0:T(8,128)(2,1)S(1)}, bf16[1024,8,128]{2,1,0:T(8,128)(2,1)}, u32[]{:S(2)}) copy-start(bf16[1024,8,128]{2,1,0:T(8,128)(2,1)} %param.21) | copy-start | bytes 6291460
  7.2 92.9 %all-gather.3.cloned.1.call-start = ((), (), s32[]{:S(2)}) async-start(), calls=%async_computation.1 | async-start | bytes 10485760 | tf_op jit(solution)/shard_map/all_gather | solution.py:34
  7.9 244.9 %all-gather.5.cloned.1.call-start = ((), (), s32[]{:S(2)}) async-start(), calls=%async_computation.2 | async-start | bytes 18874368 | tf_op jit(solution)/shard_map/all_gather | solution.py:45
  8.7 281.8 %copy-start.11 = (f32[2048]{0:T(1024)S(1)}, f32[2048]{0:T(1024)}, u32[]{:S(2)}) copy-start(f32[2048]{0:T(1024)} %param.18) | copy-start | bytes 24580
  8.7 669.9 %reduce-scatter.2.cloned.1.call-start = ((), (), s32[]{:S(2)}) async-start(), calls=%async_computation.3 | async-start | bytes 37748736 | tf_op jit(solution)/shard_map/reduce_scatter | solution.py:60
  323.9 7.4 %copy-start.5 = (bf16[1024,8,128]{2,1,0:T(8,128)(2,1)S(1)}, bf16[1024,8,128]{2,1,0:T(8,128)(2,1)}, u32[]{:S(2)}) copy-start(bf16[1024,8,128]{2,1,0:T(8,128)(2,1)} %param.22) | copy-start | bytes 6291460
  325.9 10.8 %slice-start = ((s8[8388608]{0:T(1024)(128)(4,1)}), s8[4194304]{0:T(1024)(128)(4,1)S(1)}, s32[]{:S(2)}) async-start(s8[8388608]{0:T(1024)(128)(4,1)} %bitcast.74), calls=%async_computation.4 | async-start | bytes 8388608
  325.9 10.8 %copy-start.3 = (bf16[1024,2048]{1,0:T(8,128)(2,1)S(1)}, bf16[1024,2048]{1,0:T(8,128)(2,1)}, u32[]{:S(2)}) copy-start(bf16[1024,2048]{1,0:T(8,128)(2,1)} %param.16) | copy-start | bytes 12582916
  325.9 10.8 %copy-start.4 = (bf16[1024,2048]{1,0:T(8,128)(2,1)S(1)}, bf16[1024,2048]{1,0:T(8,128)(2,1)}, u32[]{:S(2)}) copy-start(bf16[1024,2048]{1,0:T(8,128)(2,1)} %param.17) | copy-start | bytes 12582916
  325.9 10.8 %copy-start.12 = (f32[2048]{0:T(1024)S(1)}, f32[2048]{0:T(1024)}, u32[]{:S(2)}) copy-start(f32[2048]{0:T(1024)} %param.18) | copy-start | bytes 24580
  325.9 10.8 %copy-start.14 = (f32[1024]{0:T(1024)S(1)}, f32[1024]{0:T(1024)}, u32[]{:S(2)}) copy-start(f32[1024]{0:T(1024)} %get-tuple-element.211) | copy-start | bytes 12292
  372.5 10.2 %copy-start.2 = (f32[32,64,128]{2,1,0:T(8,128)S(1)}, f32[32,64,128]{2,1,0:T(8,128)}, u32[]{:S(2)}) copy-start(f32[32,64,128]{2,1,0:T(8,128)} %custom-call.1) | copy-start | bytes 3145732
  372.5 10.2 %copy-start.10 = (f32[32]{0:T(128)S(1)}, f32[32]{0:T(128)}, u32[]{:S(2)}) copy-start(f32[32]{0:T(128)} %exp.50) | copy-start | bytes 388
  382.7 138.0 %copy-start.13 = (f32[32,4]{0,1:T(4,128)S(1)}, f32[32,4]{0,1:T(4,128)}, u32[]{:S(2)}) copy-start(f32[32,4]{0,1:T(4,128)} %subtract_exponential_fusion.1) | copy-start | bytes 1540
  382.9 3.8 collective-permute-start
  387.1 20.4 %collective-permute-start = (bf16[32,64,128]{2,1,0:T(8,128)(2,1)S(1)}, bf16[32,64,128]{2,1,0:T(8,128)(2,1)S(1)}, u32[]{:S(2)}, u32[]{:S(2)}) collective-permute-start(bf16[32,64,128]{2,1,0:T(8,128)(2,1)S(1)} %fusion.76), channel_id=1, source_target_pairs={{4,0},{8,4},{12,8},{16,12},{20,16},{24,20},{28,24},{5,1},{9,5},{13... | collective-permute-start | bytes 1572872 | tf_op jit(solution)/shard_map/while/body/eval_jaxpr/ppermute | solution.py:16
  407.8 22.1 %collective-permute-start = (bf16[32,64,128]{2,1,0:T(8,128)(2,1)S(1)}, bf16[32,64,128]{2,1,0:T(8,128)(2,1)S(1)}, u32[]{:S(2)}, u32[]{:S(2)}) collective-permute-start(bf16[32,64,128]{2,1,0:T(8,128)(2,1)S(1)} %fusion.76), channel_id=1, source_target_pairs={{4,0},{8,4},{12,8},{16,12},{20,16},{24,20},{28,24},{5,1},{9,5},{13... | collective-permute-start | bytes 1572872 | tf_op jit(solution)/shard_map/while/body/eval_jaxpr/ppermute | solution.py:16
  430.3 22.3 %collective-permute-start = (bf16[32,64,128]{2,1,0:T(8,128)(2,1)S(1)}, bf16[32,64,128]{2,1,0:T(8,128)(2,1)S(1)}, u32[]{:S(2)}, u32[]{:S(2)}) collective-permute-start(bf16[32,64,128]{2,1,0:T(8,128)(2,1)S(1)} %fusion.76), channel_id=1, source_target_pairs={{4,0},{8,4},{12,8},{16,12},{20,16},{24,20},{28,24},{5,1},{9,5},{13... | collective-permute-start | bytes 1572872 | tf_op jit(solution)/shard_map/while/body/eval_jaxpr/ppermute | solution.py:16
  452.9 22.3 %collective-permute-start = (bf16[32,64,128]{2,1,0:T(8,128)(2,1)S(1)}, bf16[32,64,128]{2,1,0:T(8,128)(2,1)S(1)}, u32[]{:S(2)}, u32[]{:S(2)}) collective-permute-start(bf16[32,64,128]{2,1,0:T(8,128)(2,1)S(1)} %fusion.76), channel_id=1, source_target_pairs={{4,0},{8,4},{12,8},{16,12},{20,16},{24,20},{28,24},{5,1},{9,5},{13... | collective-permute-start | bytes 1572872 | tf_op jit(solution)/shard_map/while/body/eval_jaxpr/ppermute | solution.py:16
  475.5 22.3 %collective-permute-start = (bf16[32,64,128]{2,1,0:T(8,128)(2,1)S(1)}, bf16[32,64,128]{2,1,0:T(8,128)(2,1)S(1)}, u32[]{:S(2)}, u32[]{:S(2)}) collective-permute-start(bf16[32,64,128]{2,1,0:T(8,128)(2,1)S(1)} %fusion.76), channel_id=1, source_target_pairs={{4,0},{8,4},{12,8},{16,12},{20,16},{24,20},{28,24},{5,1},{9,5},{13... | collective-permute-start | bytes 1572872 | tf_op jit(solution)/shard_map/while/body/eval_jaxpr/ppermute | solution.py:16
  498.2 22.3 %collective-permute-start = (bf16[32,64,128]{2,1,0:T(8,128)(2,1)S(1)}, bf16[32,64,128]{2,1,0:T(8,128)(2,1)S(1)}, u32[]{:S(2)}, u32[]{:S(2)}) collective-permute-start(bf16[32,64,128]{2,1,0:T(8,128)(2,1)S(1)} %fusion.76), channel_id=1, source_target_pairs={{4,0},{8,4},{12,8},{16,12},{20,16},{24,20},{28,24},{5,1},{9,5},{13... | collective-permute-start | bytes 1572872 | tf_op jit(solution)/shard_map/while/body/eval_jaxpr/ppermute | solution.py:16
  520.7 17.2 %copy-start.9 = (pred[256,256]{1,0:T(8,128)(4,1)S(1)}, pred[256,256]{1,0:T(8,128)(4,1)}, u32[]{:S(2)}) copy-start(pred[256,256]{1,0:T(8,128)(4,1)} %iota_compare_fusion) | copy-start | bytes 196612
  520.7 17.2 %copy-start.16 = (f32[32]{0:T(128)S(1)}, f32[32]{0:T(128)}, u32[]{:S(2)}) copy-start(f32[32]{0:T(128)} %param.23) | copy-start | bytes 388
  563.8 124.8 %copy-start.1 = (bf16[1024,8,128]{2,1,0:T(8,128)(2,1)S(1)}, bf16[1024,8,128]{2,1,0:T(8,128)(2,1)}, u32[]{:S(2)}) copy-start(bf16[1024,8,128]{2,1,0:T(8,128)(2,1)} %param.21) | copy-start | bytes 6291460
  (5 other events, 15.7 us)
Sparse Core Ops, SparseCore 0:
  9.8 90.1 all-gather.2
  101.7 151.0 all-gather.4
  317.3 361.1 reduce-scatter.1
where the time goes:
time: 700 us; the launch traced here: 695 us
  waiting for transfers between devices  480 us (69%)
  matrix products  119 us (17%)
  other arithmetic  31.1 us (4%)
  local copies, waits for them, and re-layouts  30.7 us (4%)
  between operations  14.2 us (2%)
  blocking collectives  10.5 us (2%)
  starting transfers between devices  9.16 us (1%)
    all_gather x1, waiting for transfers between devices, on_device(): lax.all_gather(out_weight, 'seq', axis=0, tiled=True)  153 us
    ppermute x7, waiting for transfers between devices, shifted(): return lax.ppermute(x, axis, pairs)  126 us
    reduce_scatter x1, waiting for transfers between devices, on_device(): lax.psum_scatter(lax.dot_general(columns, normed, (((0,), (0,)), ((), ())...  108 us
    all_gather x1, waiting for transfers between devices, on_device(): full_grad = lax.all_gather(grad_output, 'head', axis=1, tiled=True)  91.3 us
    dot_general x1, matrix products, on_device(): jnp.dot(columns, lax.all_gather(out_weight, 'seq', axis=0, tiled=True), p...  27.2 us
    dot_general x1, matrix products, on_device(): lax.dot_general(columns, normed, (((0,), (0,)), ((), ())), preferred_elem...  26.7 us
    dot_general x1, matrix products, on_device(): jnp.einsum('hkts,hksp->hktp', block_weights, grad_heads, preferred_elemen...  21 us
    dot_general x1, matrix products, on_device(): jnp.einsum('hkpn,hktn->hktp', carry_low, b_heads, preferred_element_type=...  17.2 us
  transfers between devices with their start and end apart: 10, of which 10 were waited for; matrix products, arithmetic and copies ran while one was open for 16% of the time, Pallas kernels for 0%

commit v1 on v0

--- a/solution.py
+++ b/solution.py
@@ -8,6 +8,16 @@
 GROUPS = 8
 BLOCK_LEN = 256
 epsilon = 1e-05
+
+
+def turned_line(value, axis, dim):
+    size = lax.axis_size(axis)
+    block, blocks = (value, [value])
+    for _ in range(size - 1):
+        block = lax.ppermute(block, axis, [(i, (i + 1) % size) for i in range(size)])
+        blocks.insert(0, block)
+    line = jnp.concatenate(blocks, axis=dim)
+    return jnp.roll(line, (lax.axis_index(axis) + 1) * value.shape[dim], axis=dim)
 
 
 def shifted(x, axis, by):
@@ -31,7 +41,7 @@
     tok_rows = ssd_out.shape[0]
     local_width = ssd_out.shape[1]
     total_width = local_width * lax.axis_size("head")
-    full_grad = lax.all_gather(grad_output, "head", axis=1, tiled=True)
+    full_grad = turned_line(grad_output, "head", 1)
     values = ssd_out.astype(jnp.float32)
     gate_values = gate.astype(jnp.float32)
     sigmoid_gate = jax.nn.sigmoid(gate_values)

time: 700 us -> 623 us (0.89)
  waiting for transfers between devices: 480 us -> 382 us
  local copies, waits for them, and re-layouts: 30.7 us -> 44.5 us
    all_gather x1, waiting for transfers between devices: 153 us -> 0.01 us  [on_device(): lax.all_gather(out_weight, 'seq', axis=0, tiled=True)]
    ppermute x0 -> x3, waiting for transfers between devices: none -> 141 us  [turned_line(): lax.ppermute(block, axis, [(i, (i + 1) % size) for i in range(size)])]
    all_gather x1 -> x0, waiting for transfers between devices: 91.3 us -> none  [on_device(): full_grad = lax.all_gather(grad_output, 'head', axis=1, tiled=True)]
    unnamed x40 -> x46, local copies, waits for them, and re-layouts: 14.4 us -> 26.5 us
  transfers between devices with their start and end apart: 10 -> 12, of which waited for: 10 -> 11; matrix products, arithmetic and copies ran while one was open for 16% -> 21% of each run, Pallas kernels for 0% -> 0%
where the time goes in v1:
time: 623 us; the launch traced here: 618 us
  waiting for transfers between devices  382 us (61%)
  matrix products  124 us (20%)
  local copies, waits for them, and re-layouts  44.5 us (7%)
  other arithmetic  30.8 us (5%)
  between operations  14.5 us (2%)
  starting transfers between devices  12.9 us (2%)
  blocking collectives  8.16 us (1%)
    ppermute x3, waiting for transfers between devices, turned_line(): lax.ppermute(block, axis, [(i, (i + 1) % size) for i in range(size)])  141 us
    ppermute x7, waiting for transfers between devices, shifted(): return lax.ppermute(x, axis, pairs)  130 us
    reduce_scatter x1, waiting for transfers between devices, on_device(): lax.psum_scatter(lax.dot_general(columns, normed, (((0,), (0,)), ((), ())...  111 us
    dot_general x1, matrix products, on_device(): lax.dot_general(columns, normed, (((0,), (0,)), ((), ())), preferred_elem...  31.3 us
    dot_general x1, matrix products, on_device(): jnp.dot(columns, lax.all_gather(out_weight, 'seq', axis=0, tiled=True), p...  27.4 us
    unnamed x46, local copies, waits for them, and re-layouts  26.5 us
    dot_general x1, matrix products, on_device(): jnp.einsum('hkts,hksp->hktp', block_weights, grad_heads, preferred_elemen...  21 us
    dot_general x1, matrix products, on_device(): jnp.einsum('hkpn,hktn->hktp', carry_low, b_heads, preferred_element_type=...  17.2 us
  transfers between devices with their start and end apart: 12, of which 11 were waited for; matrix products, arithmetic and copies ran while one was open for 21% of the time, Pallas kernels for 0%

profile of v1, /device:TPU:0, one launch (start us, length us, event | category | flops | bytes accessed | tf_op | source)
XLA Modules:
  0.0 617.9 jit_solution(13002204339327520066)
XLA Ops:
  11.0 46.8 %collective-permute-done.1 = bf16[1024,1024]{1,0:T(8,128)(2,1)S(1)} collective-permute-done((bf16[1024,1024]{1,0:T(8,128)(2,1)}, bf16[1024,1024]{1,0:T(8,128)(2,1)S(1)}, u32[]{:S(2)}, u32[]{:S(2)}) %collective-permute-start.1) | collective-permute-done | bytes 2097184 | tf_op jit(solution)/shard_map/ppermute | solution.py:17
  59.9 47.1 %collective-permute-done.2 = bf16[1024,1024]{1,0:T(8,128)(2,1)} collective-permute-done((bf16[1024,1024]{1,0:T(8,128)(2,1)S(1)}, bf16[1024,1024]{1,0:T(8,128)(2,1)}, u32[]{:S(2)}, u32[]{:S(2)}) %collective-permute-start.2) | collective-permute-done | bytes 2097184 | tf_op jit(solution)/shard_map/ppermute | solution.py:17
  107.0 47.2 %collective-permute-done.3 = bf16[1024,1024]{1,0:T(8,128)(2,1)} collective-permute-done((bf16[1024,1024]{1,0:T(8,128)(2,1)}, bf16[1024,1024]{1,0:T(8,128)(2,1)}, u32[]{:S(2)}, u32[]{:S(2)}) %collective-permute-start.3) | collective-permute-done | bytes 2097184 | tf_op jit(solution)/shard_map/ppermute | solution.py:17
  172.7 27.4 %multiply_reduce_fusion.1 = (f32[1024]{0:T(1024)S(1)}, f32[1024]{0:T(1024)S(1)}, f32[1024,2048]{1,0:T(8,128)}) fusion(bf16[1024,2048]{1,0:T(8,128)(2,1)} %param.16, bf16[1024,2048]{1,0:T(8,128)(2,1)} %param.17, f32[2048]{0:T(1024)S(1)} %copy-done.13, bf16[4096,2048]{1,0:T(8,128)(2,1)} %all-gather.2.cloned.1.call-done, ...), kind=kOutput, calls=%fused_computation.33 | convolution fusion | flops 17205035008 | bytes 41959428 | tf_op jit(solution)/shard_map/dot_general | solution.py:53
  200.1 8.2 %all-reduce = (f32[1024]{0:T(1024)}, f32[1024]{0:T(1024)S(1)}) all-reduce(f32[1024]{0:T(1024)S(1)} %get-tuple-element.187, f32[1024]{0:T(1024)S(1)} %get-tuple-element.186), channel_id=1, replica_groups=mesh['seq'=8,'head'=4] {'head'}, use_global_device_ids=true, to_apply=%region_5.6 | all-reduce | flops 2048 | bytes 16384 | tf_op jit(solution)/shard_map/psum | solution.py:58
  208.3 31.3 %fusion.26 = f32[4096,2048]{1,0:T(8,128)} fusion(bf16[1024,8192]{1,0:T(8,128)(2,1)} %constant_dynamic-update-slice_fusion, s32[]{:T(128)S(6)} %select_n.29, bf16[1024,2048]{1,0:T(8,128)(2,1)} %param.16, f32[2048]{0:T(1024)S(1)} %copy-done.13, f32[1024]{0:T(1024)S(1)} %get-tuple-element.214, bf16[1024,2048]{1,0:T(8,128)(2,1)} %param.17), kind=kOutput, calls=%fused_computation.40 | convolution fusion | flops 17200840704 | bytes 50343940 | tf_op jit(solution)/shard_map/dot_general | solution.py:71
  248.0 5.4 convolution_convert_fusion.1
  253.4 5.2 convolution_convert_fusion
  259.4 9.2 %fusion.10 = (bf16[1024,2048]{1,0:T(8,128)(2,1)}, bf16[1024,2048]{1,0:T(8,128)(2,1)}) fusion(bf16[1024,2048]{1,0:T(8,128)(2,1)S(1)} %copy-done.6, bf16[1024,2048]{1,0:T(8,128)(2,1)S(1)} %copy-done.7, f32[1024]{0:T(1024)S(1)} %copy-done.15, f32[1024,2048]{1,0:T(8,128)S(1)} %bitcast.71, f32[1024]{0:T(1024)S(1)} %get-tuple-element.215, f32[2048]{0:T(1024)S(1)} %copy-done.14, ...), kind=kLoop, calls=%fused_computation.21 | loop fusion | flops 46137344 | bytes 25186304 | tf_op jit(solution)/shard_map/convert_element_type | solution.py:67
  268.6 6.5 %copy.43 = bf16[1024,2048]{0,1:T(8,128)(2,1)} copy(bf16[1024,2048]{1,0:T(8,128)(2,1)} %get-tuple-element.211) | data formatting | bytes 8388608 | tf_op jit(solution)/shard_map/convert_element_type | solution.py:68
  275.0 16.3 %fusion.43 = f32[4,32,64,128]{3,2,0,1:T(8,128)} fusion(bf16[32,4,256,128]{3,0,2,1:T(8,128)(2,1)} %bitcast.72, f32[32,4,256]{2,1,0:T(4,128)S(1)} %copy-done.12, bf16[32,8,4,8,256]{4,3,2,1,0:T(8,128)(2,1)} %bitcast.74), kind=kOutput, calls=%fused_computation.55 | convolution fusion | flops 543162368 | bytes 16908288 | tf_op jit(solution)/shard_map/hksp,hksn->hkpn/dot_general | solution.py:114
  293.9 10.0 %while.28 = (s32[]{:T(128)}, f32[32,64,128]{2,1,0:T(8,128)S(1)}, f32[4,32,64,128]{3,2,1,0:T(8,128)}, f32[4,32,64,128]{3,2,0,1:T(8,128)}, f32[4,32]{1,0:T(4,128)S(1)}, /*index=5*/s32[]{:T(128)}, s32[]{:T(128)}, s32[]{:T(128)}) while((s32[]{:T(128)}, f32[32,64,128]{2,1,0:T(8,128)S(1)}, f32[4,32,64,128]{3,2,1,0:T(8,128)}, ...), condition=%wide.region_7.8_spmd.clone, body=%wide.region_6.7_spmd.clone.sunk | while | flops 1048580 | bytes 5243392 | solution.py:121
  303.9 141.2 %while.29 = (s32[]{:T(128)}, f32[32,64,128]{2,1,0:T(8,128)S(1)}, f32[32]{0:T(128)S(1)}, f32[32,64,128]{2,1,0:T(8,128)S(1)}, s32[]{:T(128)}, /*index=5*/s32[]{:T(128)}) while((s32[]{:T(128)}, f32[32,64,128]{2,1,0:T(8,128)S(1)}, f32[32]{0:T(128)S(1)}, f32[32,64,128]{2,1,0:T(8,128)S(1)}, s32[]{:T(128)}, /*index=5*/s32[]{:T(128)}) %tuple.80), condition=%wide.region_11.12_spmd.clone, body=%wide.region_10.11_spmd.clone.sunk | while | flops 1310723 | bytes 6291703 | solution.py:134
  309.6 21.3 %collective-permute-done = bf16[32,64,128]{2,1,0:T(8,128)(2,1)S(1)} collective-permute-done((bf16[32,64,128]{2,1,0:T(8,128)(2,1)S(1)}, bf16[32,64,128]{2,1,0:T(8,128)(2,1)S(1)}, u32[]{:S(2)}, u32[]{:S(2)}) %collective-permute-start) | collective-permute-done | bytes 524320 | tf_op jit(solution)/shard_map/while/body/eval_jaxpr/ppermute | solution.py:26
  332.5 21.5 %collective-permute-done = bf16[32,64,128]{2,1,0:T(8,128)(2,1)S(1)} collective-permute-done((bf16[32,64,128]{2,1,0:T(8,128)(2,1)S(1)}, bf16[32,64,128]{2,1,0:T(8,128)(2,1)S(1)}, u32[]{:S(2)}, u32[]{:S(2)}) %collective-permute-start) | collective-permute-done | bytes 524320 | tf_op jit(solution)/shard_map/while/body/eval_jaxpr/ppermute | solution.py:26
  355.6 21.2 %collective-permute-done = bf16[32,64,128]{2,1,0:T(8,128)(2,1)S(1)} collective-permute-done((bf16[32,64,128]{2,1,0:T(8,128)(2,1)S(1)}, bf16[32,64,128]{2,1,0:T(8,128)(2,1)S(1)}, u32[]{:S(2)}, u32[]{:S(2)}) %collective-permute-start) | collective-permute-done | bytes 524320 | tf_op jit(solution)/shard_map/while/body/eval_jaxpr/ppermute | solution.py:26
  378.4 20.9 %collective-permute-done = bf16[32,64,128]{2,1,0:T(8,128)(2,1)S(1)} collective-permute-done((bf16[32,64,128]{2,1,0:T(8,128)(2,1)S(1)}, bf16[32,64,128]{2,1,0:T(8,128)(2,1)S(1)}, u32[]{:S(2)}, u32[]{:S(2)}) %collective-permute-start) | collective-permute-done | bytes 524320 | tf_op jit(solution)/shard_map/while/body/eval_jaxpr/ppermute | solution.py:26
  401.0 21.1 %collective-permute-done = bf16[32,64,128]{2,1,0:T(8,128)(2,1)S(1)} collective-permute-done((bf16[32,64,128]{2,1,0:T(8,128)(2,1)S(1)}, bf16[32,64,128]{2,1,0:T(8,128)(2,1)S(1)}, u32[]{:S(2)}, u32[]{:S(2)}) %collective-permute-start) | collective-permute-done | bytes 524320 | tf_op jit(solution)/shard_map/while/body/eval_jaxpr/ppermute | solution.py:26
  423.7 21.1 %collective-permute-done = bf16[32,64,128]{2,1,0:T(8,128)(2,1)S(1)} collective-permute-done((bf16[32,64,128]{2,1,0:T(8,128)(2,1)S(1)}, bf16[32,64,128]{2,1,0:T(8,128)(2,1)S(1)}, u32[]{:S(2)}, u32[]{:S(2)}) %collective-permute-start) | collective-permute-done | bytes 524320 | tf_op jit(solution)/shard_map/while/body/eval_jaxpr/ppermute | solution.py:26
  445.1 17.2 %fusion.22 = f32[32,4,256,64]{2,3,1,0:T(8,128)} fusion(bf16[32,4,256,128]{3,0,2,1:T(8,128)(2,1)} %bitcast.67, f32[4,32,64,128]{3,2,1,0:T(8,128)} %get-tuple-element.129, f32[32,64,128]{2,1,0:T(8,128)S(1)} %get-tuple-element.131, f32[32,4]{0,1:T(4,128)S(1)} %subtract_exponential_fusion.1), kind=kOutput, calls=%fused_computation.37 | convolution fusion | flops 540016640 | bytes 22020608 | tf_op jit(solution)/shard_map/hkpn,hktn->hktp/dot_general | solution.py:137
  462.3 21.0 %fusion.48 = bf16[32,4,8,8,256]{4,3,2,1,0:T(8,128)(2,1)} fusion(bf16[32,8,4,8,256]{4,3,2,1,0:T(8,128)(2,1)} %bitcast.75, f32[32]{0:T(128)S(1)} %copy-done.16, f32[32,4,256,64]{2,3,1,0:T(8,128)} %fusion.22, f32[32,4,256]{2,1,0:T(4,128)S(1)} %copy.51, f32[32,4,256]{2,1,0:T(4,128)S(1)} %copy.41, pred[256,256]{1,0:T(8,128)(4,1)S(1)} %iota_compare_fusion, ...), kind=kOutput, calls=%fused_computation.56 | convolution fusion | flops 3277848576 | bytes 34013312 | tf_op jit(solution)/shard_map/hkts,hksp->hktp/dot_general | solution.py:109
  488.2 6.6 %copy.53 = bf16[1024,2048]{1,0:T(8,128)(2,1)} copy(bf16[1024,2048]{0,1:T(8,128)(2,1)} %bitcast.69) | data formatting | bytes 8388608
  494.8 111.0 %reduce-scatter.2.cloned.1.call-done = f32[512,2048]{1,0:T(8,128)} async-done(((f32[4096,2048]{1,0:T(8,128)}), f32[512,2048]{1,0:T(8,128)}) %reduce-scatter.2.cloned.1.call-update) | async-done | bytes 4194320 | tf_op jit(solution)/shard_map/reduce_scatter | solution.py:70
  605.8 5.0 broadcast_multiply_fusion
  (112 shorter events, 64.3 us)
Async XLA Ops:
  7.2 240.8 %copy-start = (bf16[1024,8,128]{2,1,0:T(8,128)(2,1)S(1)}, bf16[1024,8,128]{2,1,0:T(8,128)(2,1)}, u32[]{:S(2)}) copy-start(bf16[1024,8,128]{2,1,0:T(8,128)(2,1)} %param.21) | copy-start | bytes 6291460
  7.2 165.5 %all-gather.2.cloned.1.call-start = ((), (), s32[]{:S(2)}) async-start(), calls=%async_computation.1 | async-start | bytes 18874368 | tf_op jit(solution)/shard_map/all_gather | solution.py:55
  7.9 597.9 %reduce-scatter.2.cloned.1.call-start = ((), (), s32[]{:S(2)}) async-start(), calls=%async_computation.2 | async-start | bytes 37748736 | tf_op jit(solution)/shard_map/reduce_scatter | solution.py:70
  8.0 49.8 %collective-permute-start.1 = (bf16[1024,1024]{1,0:T(8,128)(2,1)}, bf16[1024,1024]{1,0:T(8,128)(2,1)S(1)}, u32[]{:S(2)}, u32[]{:S(2)}) collective-permute-start(bf16[1024,1024]{1,0:T(8,128)(2,1)} %param.14), channel_id=1, source_target_pairs={{0,1},{1,2},{2,3},{3,0},{4,5},{5,6},{6,7},{7,4},{8,9},{9,10},{10,1... | collective-permute-start | bytes 6291464 | tf_op jit(solution)/shard_map/ppermute | solution.py:17
  59.1 47.9 %collective-permute-start.2 = (bf16[1024,1024]{1,0:T(8,128)(2,1)S(1)}, bf16[1024,1024]{1,0:T(8,128)(2,1)}, u32[]{:S(2)}, u32[]{:S(2)}) collective-permute-start(bf16[1024,1024]{1,0:T(8,128)(2,1)S(1)} %collective-permute-done.1), channel_id=1, source_target_pairs={{0,1},{1,2},{2,3},{3,0},{4,5},{5,6},{6,7},{7,4},{8,9},{9,10},{10,1... | collective-permute-start | bytes 6291464 | tf_op jit(solution)/shard_map/ppermute | solution.py:17
  107.0 47.3 %collective-permute-start.3 = (bf16[1024,1024]{1,0:T(8,128)(2,1)}, bf16[1024,1024]{1,0:T(8,128)(2,1)}, u32[]{:S(2)}, u32[]{:S(2)}) collective-permute-start(bf16[1024,1024]{1,0:T(8,128)(2,1)} %collective-permute-done.2), channel_id=1, source_target_pairs={{0,1},{1,2},{2,3},{3,0},{4,5},{5,6},{6,7},{7,4},{8,9},{9,10},{10,1... | collective-permute-start | bytes 6291464 | tf_op jit(solution)/shard_map/ppermute | solution.py:17
  107.0 53.5 %copy-start.5 = (bf16[1024,1024]{1,0:T(8,128)(2,1)S(1)}, bf16[1024,1024]{1,0:T(8,128)(2,1)}, u32[]{:S(2)}) copy-start(bf16[1024,1024]{1,0:T(8,128)(2,1)} %copy-done.4) | copy-start | bytes 6291460
  107.0 55.0 %copy-start.3 = (bf16[1024,1024]{1,0:T(8,128)(2,1)S(1)}, bf16[1024,1024]{1,0:T(8,128)(2,1)}, u32[]{:S(2)}) copy-start(bf16[1024,1024]{1,0:T(8,128)(2,1)} %param.14) | copy-start | bytes 6291460
  247.9 10.7 %slice-start = ((s8[8388608]{0:T(1024)(128)(4,1)}), s8[4194304]{0:T(1024)(128)(4,1)S(1)}, s32[]{:S(2)}) async-start(s8[8388608]{0:T(1024)(128)(4,1)} %bitcast.70), calls=%async_computation.3 | async-start | bytes 8388608
  247.9 10.7 %copy-start.6 = (bf16[1024,2048]{1,0:T(8,128)(2,1)S(1)}, bf16[1024,2048]{1,0:T(8,128)(2,1)}, u32[]{:S(2)}) copy-start(bf16[1024,2048]{1,0:T(8,128)(2,1)} %param.16) | copy-start | bytes 12582916
  248.0 10.7 %copy-start.7 = (bf16[1024,2048]{1,0:T(8,128)(2,1)S(1)}, bf16[1024,2048]{1,0:T(8,128)(2,1)}, u32[]{:S(2)}) copy-start(bf16[1024,2048]{1,0:T(8,128)(2,1)} %param.17) | copy-start | bytes 12582916
  248.0 10.7 %copy-start.14 = (f32[2048]{0:T(1024)S(1)}, f32[2048]{0:T(1024)}, u32[]{:S(2)}) copy-start(f32[2048]{0:T(1024)} %param.18) | copy-start | bytes 24580
  248.0 10.7 %copy-start.15 = (f32[1024]{0:T(1024)S(1)}, f32[1024]{0:T(1024)}, u32[]{:S(2)}) copy-start(f32[1024]{0:T(1024)} %get-tuple-element.208) | copy-start | bytes 12292
  293.9 10.0 %copy-start.2 = (f32[32,64,128]{2,1,0:T(8,128)S(1)}, f32[32,64,128]{2,1,0:T(8,128)}, u32[]{:S(2)}) copy-start(f32[32,64,128]{2,1,0:T(8,128)} %custom-call.1) | copy-start | bytes 3145732
  304.1 3.8 collective-permute-start
  308.3 22.6 %collective-permute-start = (bf16[32,64,128]{2,1,0:T(8,128)(2,1)S(1)}, bf16[32,64,128]{2,1,0:T(8,128)(2,1)S(1)}, u32[]{:S(2)}, u32[]{:S(2)}) collective-permute-start(bf16[32,64,128]{2,1,0:T(8,128)(2,1)S(1)} %fusion.80), channel_id=1, source_target_pairs={{4,0},{8,4},{12,8},{16,12},{20,16},{24,20},{28,24},{5,1},{9,5},{13... | collective-permute-start | bytes 1572872 | tf_op jit(solution)/shard_map/while/body/eval_jaxpr/ppermute | solution.py:26
  331.2 22.8 %collective-permute-start = (bf16[32,64,128]{2,1,0:T(8,128)(2,1)S(1)}, bf16[32,64,128]{2,1,0:T(8,128)(2,1)S(1)}, u32[]{:S(2)}, u32[]{:S(2)}) collective-permute-start(bf16[32,64,128]{2,1,0:T(8,128)(2,1)S(1)} %fusion.80), channel_id=1, source_target_pairs={{4,0},{8,4},{12,8},{16,12},{20,16},{24,20},{28,24},{5,1},{9,5},{13... | collective-permute-start | bytes 1572872 | tf_op jit(solution)/shard_map/while/body/eval_jaxpr/ppermute | solution.py:26
  354.3 22.5 %collective-permute-start = (bf16[32,64,128]{2,1,0:T(8,128)(2,1)S(1)}, bf16[32,64,128]{2,1,0:T(8,128)(2,1)S(1)}, u32[]{:S(2)}, u32[]{:S(2)}) collective-permute-start(bf16[32,64,128]{2,1,0:T(8,128)(2,1)S(1)} %fusion.80), channel_id=1, source_target_pairs={{4,0},{8,4},{12,8},{16,12},{20,16},{24,20},{28,24},{5,1},{9,5},{13... | collective-permute-start | bytes 1572872 | tf_op jit(solution)/shard_map/while/body/eval_jaxpr/ppermute | solution.py:26
  377.1 22.2 %collective-permute-start = (bf16[32,64,128]{2,1,0:T(8,128)(2,1)S(1)}, bf16[32,64,128]{2,1,0:T(8,128)(2,1)S(1)}, u32[]{:S(2)}, u32[]{:S(2)}) collective-permute-start(bf16[32,64,128]{2,1,0:T(8,128)(2,1)S(1)} %fusion.80), channel_id=1, source_target_pairs={{4,0},{8,4},{12,8},{16,12},{20,16},{24,20},{28,24},{5,1},{9,5},{13... | collective-permute-start | bytes 1572872 | tf_op jit(solution)/shard_map/while/body/eval_jaxpr/ppermute | solution.py:26
  399.7 22.4 %collective-permute-start = (bf16[32,64,128]{2,1,0:T(8,128)(2,1)S(1)}, bf16[32,64,128]{2,1,0:T(8,128)(2,1)S(1)}, u32[]{:S(2)}, u32[]{:S(2)}) collective-permute-start(bf16[32,64,128]{2,1,0:T(8,128)(2,1)S(1)} %fusion.80), channel_id=1, source_target_pairs={{4,0},{8,4},{12,8},{16,12},{20,16},{24,20},{28,24},{5,1},{9,5},{13... | collective-permute-start | bytes 1572872 | tf_op jit(solution)/shard_map/while/body/eval_jaxpr/ppermute | solution.py:26
  422.4 22.4 %collective-permute-start = (bf16[32,64,128]{2,1,0:T(8,128)(2,1)S(1)}, bf16[32,64,128]{2,1,0:T(8,128)(2,1)S(1)}, u32[]{:S(2)}, u32[]{:S(2)}) collective-permute-start(bf16[32,64,128]{2,1,0:T(8,128)(2,1)S(1)} %fusion.80), channel_id=1, source_target_pairs={{4,0},{8,4},{12,8},{16,12},{20,16},{24,20},{28,24},{5,1},{9,5},{13... | collective-permute-start | bytes 1572872 | tf_op jit(solution)/shard_map/while/body/eval_jaxpr/ppermute | solution.py:26
  445.1 17.3 %copy-start.11 = (f32[32,4,256]{2,1,0:T(4,128)S(1)}, f32[32,4,256]{2,1,0:T(4,128)}, u32[]{:S(2)}) copy-start(f32[32,4,256]{2,1,0:T(4,128)} %mul.168) | copy-start | bytes 393220
  445.1 17.3 %copy-start.16 = (f32[32]{0:T(128)S(1)}, f32[32]{0:T(128)}, u32[]{:S(2)}) copy-start(f32[32]{0:T(128)} %param.23) | copy-start | bytes 388
  488.2 122.6 %copy-start.1 = (bf16[1024,8,128]{2,1,0:T(8,128)(2,1)S(1)}, bf16[1024,8,128]{2,1,0:T(8,128)(2,1)}, u32[]{:S(2)}) copy-start(bf16[1024,8,128]{2,1,0:T(8,128)(2,1)} %param.21) | copy-start | bytes 6291460
  (7 other events, 37.0 us)
Sparse Core Ops, SparseCore 0:
  9.6 153.7 all-gather.1
  239.7 366.0 reduce-scatter.1
